TPU v7x, 32 devices: a whole 2x2x4 slice. The times are simulated.
32 devices in a mesh: grp: 8 (over z, core), sp: 4 (over y, x).
Axes of the slice: x: 2, y: 2, z: 4, core: 2. Of those that a mesh axis runs over, the one named last changes fastest.
Arguments:
- acts: bfloat16 [32, 4, 16, 728], P('grp', 'sp'), may hold values from -6 to 6
- cotangent: bfloat16 [32, 4, 16, 728], P(('grp', 'sp')), may hold values from -6 to 6
- depth_kernel: float32 [3, 3, 728], replicated, may hold values from -2 to 2
- point_weight: bfloat16 [728, 728], replicated, may hold values from -0.21875 to 0.21875
- batch_norm_gain: float32 [728], replicated, may hold values from 0.5 to 2
- norm_shift_bias: float32 [728], replicated, may hold values from -1 to 1
Outputs:
- block_out: bfloat16 [32, 4, 16, 728], P(('grp', 'sp'))
- input_grad: bfloat16 [32, 4, 16, 728], P('grp', 'sp')
- weight_grad: float32 [529984], P('sp')
All inputs are finite; a program needn't handle non-finite values.
Results may differ from a plain program's by a relative error of at most 0.018.
Values may be sent and summed in bfloat16 or wider, within the bound.
A program may use at most 64 MiB of HBM per device.

v0:
```python
import jax
import jax.numpy as jnp
from jax import lax
from jax.sharding import PartitionSpec as P


def depth_forward(field, filter_weight):
    rows = field.shape[1]
    cols = field.shape[2]
    padded = jnp.pad(field, ((0, 0), (1, 1), (1, 1), (0, 0)))
    total = jnp.zeros(field.shape, jnp.float32)
    for i in range(3):
        for j in range(3):
            total = total + padded[:, i : i + rows, j : j + cols, :] * filter_weight[i, j]
    return total


def depth_backward(field, filter_weight):
    rows = field.shape[1]
    cols = field.shape[2]
    padded = jnp.pad(field, ((0, 0), (1, 1), (1, 1), (0, 0)))
    total = jnp.zeros(field.shape, jnp.float32)
    for i in range(3):
        for j in range(3):
            total = (
                total
                + padded[:, 2 - i : 2 - i + rows, 2 - j : 2 - j + cols, :] * filter_weight[i, j]
            )
    return total


def body(acts, cotangent, depth_kernel, point_weight, batch_norm_gain, norm_shift_bias):
    channel_count = acts.shape[-1]
    sample_image = lax.all_to_all(acts, "sp", split_axis=0, concat_axis=1, tiled=True)
    input_single_precision = sample_image.astype(jnp.float32)
    hidden = jnp.maximum(input_single_precision, 0.0)
    depthed = depth_forward(hidden, depth_kernel).astype(jnp.bfloat16)
    flat_d = depthed.reshape(-1, channel_count)
    element_count = flat_d.shape[0] * lax.axis_size("sp")
    projected_output = jnp.dot(flat_d, point_weight, preferred_element_type=jnp.float32)
    total, squares = lax.psum(
        (jnp.sum(projected_output, axis=0), jnp.sum(projected_output * projected_output, axis=0)),
        "sp",
    )
    batch_mean = total / element_count
    var = squares / element_count - batch_mean * batch_mean
    inverse_deviation = lax.rsqrt(var + 1e-05)
    normalized_input = (projected_output - batch_mean) * inverse_deviation
    block_out = (
        (
            input_single_precision.reshape(-1, channel_count)
            + batch_norm_gain * normalized_input
            + norm_shift_bias
        )
        .astype(jnp.bfloat16)
        .reshape(sample_image.shape)
    )
    gfloat = cotangent.astype(jnp.float32).reshape(-1, channel_count)
    scaled_output = gfloat * batch_norm_gain
    leading_layer, second_layer = lax.psum(
        (jnp.sum(scaled_output, axis=0), jnp.sum(scaled_output * normalized_input, axis=0)), "sp"
    )
    projected_gradient = (
        inverse_deviation
        * (
            scaled_output
            - leading_layer / element_count
            - normalized_input * (second_layer / element_count)
        )
    ).astype(jnp.bfloat16)
    local_weight = jnp.dot(
        flat_d.T, projected_gradient, preferred_element_type=jnp.float32
    ).reshape(-1)
    ddepth = jnp.dot(
        projected_gradient, point_weight.T, preferred_element_type=jnp.float32
    ).reshape(sample_image.shape)
    dhidden = depth_backward(ddepth, depth_kernel)
    dinput = (
        gfloat.reshape(sample_image.shape) + jnp.where(sample_image > 0, dhidden, 0.0)
    ).astype(jnp.bfloat16)
    input_grad = lax.all_to_all(dinput, "sp", split_axis=1, concat_axis=0, tiled=True)
    slices = lax.psum_scatter(
        local_weight.astype(jnp.bfloat16), "sp", scatter_dimension=0, tiled=True
    ).astype(jnp.float32)
    weight_grad = lax.psum(slices, "grp")
    return (block_out, input_grad, weight_grad)


def solution(mesh):
    in_specs = (P("grp", "sp", None, None), P(("grp", "sp"), None, None, None), P(), P(), P(), P())
    out_specs = (P(("grp", "sp"), None, None, None), P("grp", "sp", None, None), P("sp"))
    return jax.shard_map(body, mesh=mesh, in_specs=in_specs, out_specs=out_specs, check_vma=False)
```

profile of v0, /device:TPU:0, one launch (start us, length us, event | category | flops | bytes accessed | tf_op | source)
XLA Modules:
  0.0 160.6 jit_solution(10437990497592473162)
XLA Ops:
  7.2 0.0 copy-start
  7.2 5.3 %all-to-all-start = ((bf16[4,1,16,728]{3,2,1,0:T(8,128)(2,1)}), bf16[4,1,16,728]{3,2,1,0:T(8,128)(2,1)S(1)}, u32[]{:S(2)}, u32[]{:S(2)}) async-start(bf16[4,1,16,728]{3,2,1,0:T(8,128)(2,1)} %param.6), calls=%async_computation | async-start | bytes 196608 | tf_op jit(solution)/shard_map/all_to_all | solution.py:34
  12.5 0.0 all-reduce.10.cloned.1.call-start
  12.6 1.0 multiply_reduce_fusion.1
  13.5 1.0 slice_reduce_fusion.8
  14.5 3.0 %all-to-all-done = bf16[4,1,16,728]{3,2,1,0:T(8,128)(2,1)S(1)} async-done(((bf16[4,1,16,728]{3,2,1,0:T(8,128)(2,1)}), bf16[4,1,16,728]{3,2,1,0:T(8,128)(2,1)S(1)}, u32[]{:S(2)}, u32[]{:S(2)}) %all-to-all-start) | async-done | bytes 93216 | tf_op jit(solution)/shard_map/all_to_all | solution.py:34
  17.5 0.1 fusion.9
  17.6 0.0 copy-start.3
  17.6 0.0 copy-done
  17.6 0.3 fusion.39
  18.0 8.4 %all-reduce.4 = (f32[728]{0:T(1024)S(1)}, f32[728]{0:T(1024)S(1)}) all-reduce(f32[728]{0:T(1024)S(1)} %get-tuple-element.7, f32[728]{0:T(1024)S(1)} %get-tuple-element.6), channel_id=1, replica_groups=mesh['grp'=8,'sp'=4] {'sp'}, use_global_device_ids=true, to_apply=%region_3.4 | all-reduce | flops 1456 | bytes 11648 | tf_op jit(solution)/shard_map/psum | solution.py:41
  26.5 0.0 copy-done.1
  26.5 0.0 copy-done.2
  26.5 0.1 multiply_reduce_fusion
  26.5 9.0 %all-reduce.3 = (f32[728]{0:T(1024)S(1)}, f32[728]{0:T(1024)S(1)}) all-reduce(f32[728]{0:T(1024)S(1)} %multiply_reduce_fusion, f32[728]{0:T(1024)S(1)} %multiply_reduce_fusion.1), channel_id=1, replica_groups=mesh['grp'=8,'sp'=4] {'sp'}, use_global_device_ids=true, to_apply=%region_7.8 | all-reduce | flops 1456 | bytes 11648 | tf_op jit(solution)/shard_map/psum | solution.py:60
  35.6 0.0 copy-done.3
  35.6 0.7 multiply_convert_fusion
  36.3 0.5 convolution_convert_fusion
  36.8 0.0 copy-start.4
  36.8 3.5 %convert_element_type.59 = bf16[529984]{0:T(1024)(128)(2,1)} reshape(bf16[728,728]{1,0:T(8,128)(2,1)S(1)} %convolution_convert_fusion) | data formatting | bytes 2119936 | tf_op jit(solution)/shard_map/convert_element_type | solution.py:83
  40.3 0.0 all-reduce.10.cloned.1.call-update
  40.3 0.0 all-reduce.8.cloned.1.call-start
  40.3 0.6 dynamic-slice
  41.6 0.5 fusion.40
  42.1 51.5 %all-reduce.10.cloned.1.call-done = bf16[529984]{0:T(1024)(128)(2,1)} async-done(((bf16[529984]{0:T(1024)(128)(2,1)}), bf16[529984]{0:T(1024)(128)(2,1)}) %all-reduce.10.cloned.1.call-update) | async-done | bytes 1059984
  93.5 1.9 %dynamic-slice_convert_fusion = f32[132496]{0:T(1024)} fusion(bf16[529984]{0:T(1024)(128)(2,1)} %all-reduce.10.cloned.1.call-done, u32[]{:T(128)S(6)} %multiply.5), kind=kLoop, calls=%fused_computation.17 | loop fusion | flops 132496 | bytes 794980 | tf_op jit(solution)/shard_map/convert_element_type | solution.py:84
  95.5 0.0 all-reduce.8.cloned.1.call-update
  95.5 0.2 fusion.38
  95.7 7.7 %all_to_all.21 = bf16[1,4,16,728]{3,2,0,1:T(8,128)(2,1)S(1)} all-to-all(bf16[1,4,16,728]{3,2,0,1:T(8,128)(2,1)S(1)} %fusion.38), channel_id=1, replica_groups=mesh['grp'=8,'sp'=4] {'sp'}, dimensions={1} | all-to-all | bytes 186368 | tf_op jit(solution)/shard_map/all_to_all | solution.py:81
  103.4 47.9 %all-reduce.8.cloned.1.call-done = f32[132496]{0:T(1024)} async-done(((f32[132496]{0:T(1024)}), f32[132496]{0:T(1024)}) %all-reduce.8.cloned.1.call-update) | async-done | bytes 530000 | tf_op jit(solution)/shard_map/psum | solution.py:85
  151.3 0.6 copy.16
  151.9 1.9 %copy.17 = f32[132496]{0:T(1024)} copy(f32[132496]{0:T(1024)} %all-reduce.8.cloned.1.call-done) | data formatting | bytes 1059968
  (7 shorter events, 0.1 us)
Async XLA Ops:
  7.2 10.5 %copy-start = (bf16[728,728]{1,0:T(8,128)(2,1)S(1)}, bf16[728,728]{1,0:T(8,128)(2,1)}, u32[]{:S(2)}) copy-start(bf16[728,728]{1,0:T(8,128)(2,1)} %param.9) | copy-start | bytes 3179908
  7.2 10.3 %all-to-all-start = ((bf16[4,1,16,728]{3,2,1,0:T(8,128)(2,1)}), bf16[4,1,16,728]{3,2,1,0:T(8,128)(2,1)S(1)}, u32[]{:S(2)}, u32[]{:S(2)}) async-start(bf16[4,1,16,728]{3,2,1,0:T(8,128)(2,1)} %param.6), calls=%async_computation | async-start | bytes 196608 | tf_op jit(solution)/shard_map/all_to_all | solution.py:34
  12.5 13.9 %copy-start.1 = (bf16[1,4,16,728]{3,2,1,0:T(8,128)(2,1)S(1)}, bf16[1,4,16,728]{3,2,1,0:T(8,128)(2,1)}, u32[]{:S(2)}) copy-start(bf16[1,4,16,728]{3,2,1,0:T(8,128)(2,1)} %param.7) | copy-start | bytes 279556
  12.5 13.9 %copy-start.2 = (f32[728]{0:T(1024)S(1)}, f32[728]{0:T(1024)}, u32[]{:S(2)}) copy-start(f32[728]{0:T(1024)} %param.10) | copy-start | bytes 8740
  12.5 81.0 %all-reduce.10.cloned.1.call-start = ((), (), s32[]{:S(2)}) async-start(), calls=%async_computation.3 | async-start | bytes 2121728
  17.6 18.0 %copy-start.3 = (f32[728]{0:T(1024)S(1)}, f32[728]{0:T(1024)}, u32[]{:S(2)}) copy-start(f32[728]{0:T(1024)} %param.11) | copy-start | bytes 8740
  36.8 3.5 %copy-start.4 = (u32[32]{0:T(128)S(1)}, u32[32]{0:T(128)}, u32[]{:S(2)}) copy-start(u32[32]{0:T(128)} %constant.23) | copy-start | bytes 388
  40.3 111.0 %all-reduce.8.cloned.1.call-start = ((), (), s32[]{:S(2)}) async-start(), calls=%async_computation.2 | async-start | bytes 1064960 | tf_op jit(solution)/shard_map/psum | solution.py:85
Sparse Core Ops, SparseCore 0:
  40.4 53.0 all-reduce.9
  96.5 54.7 all-reduce.7
where the time goes:
time: 161 us
  waiting for transfers between devices  102 us (63%)
  blocking collectives  25.1 us (16%)
  between operations  14.8 us (9%)
  local copies, waits for them, and re-layouts  7.53 us (5%)
  starting transfers between devices  5.41 us (3%)
  other arithmetic  4.04 us (3%)
    unnamed x3, waiting for transfers between devices  51.5 us
    psum x1, waiting for transfers between devices, body(): weight_grad = lax.psum(slices, 'grp')  47.9 us
    psum x1, blocking collectives, body(): lax.psum((jnp.sum(scaled_output, axis=0), jnp.sum(scaled_output * normali...  8.99 us
    psum x1, blocking collectives, body(): lax.psum((jnp.sum(projected_output, axis=0), jnp.sum(projected_output * p...  8.45 us
    all_to_all x1, blocking collectives, body(): lax.all_to_all(dinput, 'sp', split_axis=1, concat_axis=0, tiled=True)  7.68 us
    all_to_all x1, starting transfers between devices, body(): lax.all_to_all(acts, 'sp', split_axis=0, concat_axis=1, tiled=True)  5.34 us
    convert_element_type x1, local copies, waits for them, and re-layouts, body(): local_weight.astype(jnp.bfloat16)  3.46 us
  transfers between devices with their start and end apart: 3, of which 3 were waited for; matrix products, arithmetic and copies ran while one was open for 2% of the time, Pallas kernels for 0%

commit v1 on v0

--- a/solution.py
+++ b/solution.py
@@ -1,7 +1,293 @@
+import functools
+
 import jax
 import jax.numpy as jnp
 from jax import lax
+from jax.experimental import pallas as pl
+from jax.experimental.pallas import tpu as pltpu
 from jax.sharding import PartitionSpec as P
+
+MESH = pl.DeviceIdType.MESH
+LANES = 128
+NT = (((1,), (1,)), ((), ()))
+
+
+def lane_blocks(channels):
+    return [slice(at, min(at + LANES, channels)) for at in range(0, channels, LANES)]
+
+
+def column_shift(field, step):
+    cols = field.shape[0]
+    at = lax.broadcasted_iota(jnp.int32, field.shape, 0)
+    keep = (at >= 1) if step > 0 else (at < cols - 1)
+    return jnp.where(keep, pltpu.roll(field, step % cols, 0), 0.0)
+
+
+def kernel(
+    n_sp, n_grp, n_core, part_rows,
+    acts_ref, cot_ref, dk_ref, pw_hbm, gain_ref, bias_ref,
+    block_out_ref, input_grad_ref, weight_ref,
+    ga, gc, pw, d_ref, p_ref, dp_ref, dsel_ref, dd_ref,
+    pair_send, pair_recv, own_ref, z_send, z_recv, res_ref,
+    local_sem, a_send, a_recv, c_send, c_recv,
+    pair_ssem, pair_rsem, z_ssem, z_rsem, g_ssem, g_rsem, f_ssem, f_rsem,
+):
+    sp = lax.axis_index("sp")
+    grp = lax.axis_index("grp")
+    n_z = n_grp // n_core
+    z, core = grp // n_core, grp % n_core
+    other = (core + 1) % n_core
+    partner = z * n_core + other
+    n_rows, n_samples, cols, channels = ga.shape
+    count = n_rows * n_samples * cols
+    blocks = lane_blocks(channels)
+
+    load_pw = pltpu.make_async_copy(pw_hbm, pw, local_sem.at[0])
+    load_pw.start()
+    own_acts = pltpu.make_async_copy(acts_ref.at[:, 0], ga.at[sp], local_sem.at[1])
+    own_acts.start()
+    own_cot = pltpu.make_async_copy(cot_ref.at[0], gc.at[sp], local_sem.at[2])
+    own_cot.start()
+
+    barrier = pltpu.get_barrier_semaphore()
+    peers = [{"sp": (sp + k) % n_sp} for k in range(1, n_sp)]
+    peers += [{"grp": ((z + k) % n_z) * n_core + core} for k in range(1, n_z)]
+    peers += [{"grp": partner}]
+    for peer in peers:
+        pl.semaphore_signal(barrier, inc=1, device_id=peer, device_id_type=MESH)
+    pl.semaphore_wait(barrier, len(peers))
+
+    def acts_copy(k, slot, to):
+        return pltpu.make_async_remote_copy(
+            src_ref=acts_ref.at[:, 0], dst_ref=ga.at[slot],
+            send_sem=a_send.at[k], recv_sem=a_recv.at[slot],
+            device_id={"sp": to}, device_id_type=MESH,
+        )
+
+    def cot_copy(k, slot, to):
+        return pltpu.make_async_remote_copy(
+            src_ref=cot_ref.at[0], dst_ref=gc.at[slot],
+            send_sem=c_send.at[k], recv_sem=c_recv.at[slot],
+            device_id={"sp": to}, device_id_type=MESH,
+        )
+
+    for k in range(1, n_sp):
+        acts_copy(k, sp, (sp + k) % n_sp).start()
+    for k in range(1, n_sp):
+        cot_copy(k, sp, (sp + k) % n_sp).start()
+
+    dp_ref[0] = jnp.zeros(dp_ref.shape[1:], dp_ref.dtype)
+    dp_ref[n_rows + 1] = jnp.zeros(dp_ref.shape[1:], dp_ref.dtype)
+    own_acts.wait()
+    load_pw.wait()
+    for k in range(1, n_sp):
+        acts_copy(k, (sp + k) % n_sp, sp).wait_recv()
+
+    @pl.loop(0, n_samples)
+    def _(b):
+        for lanes in blocks:
+            h = [jnp.maximum(ga[r, b, :, lanes].astype(jnp.float32), 0.0) for r in range(n_rows)]
+            taps = [[dk_ref[i, j : j + 1, lanes] for j in range(3)] for i in range(3)]
+            for r in range(n_rows):
+                t = [
+                    sum(h[r + i - 1] * taps[i][j] for i in range(3) if 0 <= r + i - 1 < n_rows)
+                    for j in range(3)
+                ]
+                total = t[1] + column_shift(t[0], 1) + column_shift(t[2], -1)
+                at = pl.multiple_of((r * n_samples + b) * cols, cols)
+                d_ref[pl.ds(at, cols), lanes] = total.astype(jnp.bfloat16)
+
+    p_ref[...] = jnp.dot(
+        d_ref[...], pw[...], preferred_element_type=jnp.float32
+    ).reshape(p_ref.shape)
+    sel_rows = dsel_ref.shape[0]
+    width = channels // n_sp
+    row = lax.broadcasted_iota(jnp.int32, (sel_rows, channels), 0)
+    lane = lax.broadcasted_iota(jnp.int32, (sel_rows, channels), 1)
+    pick = jnp.where((lane - sp * width == row) & (row < width), 1.0, 0.0).astype(jnp.bfloat16)
+    dsel_ref[...] = lax.dot_general(
+        pick, d_ref[...], NT, preferred_element_type=jnp.float32
+    ).astype(jnp.bfloat16)
+
+    own_cot.wait()
+    for k in range(1, n_sp):
+        cot_copy(k, (sp + k) % n_sp, sp).wait_recv()
+
+    means, rstds = [], []
+    for lanes in blocks:
+        size = lanes.stop - lanes.start
+        s1 = s2 = sg = sgp = jnp.zeros((cols, size), jnp.float32)
+        for r in range(n_rows):
+            for b in range(n_samples):
+                p = p_ref[r, b * cols : (b + 1) * cols, lanes]
+                g = gc[b, r, :, lanes].astype(jnp.float32)
+                s1, s2, sg, sgp = s1 + p, s2 + p * p, sg + g, sgp + g * p
+        s1, s2, sg, sgp = [jnp.sum(s, axis=0, keepdims=True) for s in (s1, s2, sg, sgp)]
+        gain = gain_ref[:, lanes]
+        mean = s1 / count
+        var = s2 / count - mean * mean
+        rstd = lax.rsqrt(var + 1e-05)
+        a1 = gain * sg / count
+        a2 = gain * rstd * (sgp - mean * sg) / count
+        means.append(mean)
+        rstds.append(rstd)
+        for r in range(n_rows):
+            for b in range(n_samples):
+                p = p_ref[r, b * cols : (b + 1) * cols, lanes]
+                g = gc[b, r, :, lanes].astype(jnp.float32)
+                xhat = (p - mean) * rstd
+                dp_ref[r + 1, b * cols : (b + 1) * cols, lanes] = (
+                    rstd * (g * gain - a1 - xhat * a2)
+                ).astype(jnp.bfloat16)
+
+    half = n_z * part_rows
+
+    def product(which):
+        left = dsel_ref[pl.ds(pl.multiple_of(which * half, half), half), :]
+        return jnp.dot(
+            left, dp_ref[1 : n_rows + 1].reshape(-1, channels), preferred_element_type=jnp.float32
+        ).reshape(n_z, part_rows, channels)
+
+    def pair_copy(k):
+        return pltpu.make_async_remote_copy(
+            src_ref=pair_send.at[k], dst_ref=pair_recv.at[k],
+            send_sem=pair_ssem.at[k], recv_sem=pair_rsem.at[k],
+            device_id={"grp": partner}, device_id_type=MESH,
+        )
+
+    def z_copy(k, slot, to):
+        return pltpu.make_async_remote_copy(
+            src_ref=z_send.at[k], dst_ref=z_recv.at[slot],
+            send_sem=z_ssem.at[k], recv_sem=z_rsem.at[slot],
+            device_id={"grp": to * n_core + core}, device_id_type=MESH,
+        )
+
+    def gather_copy(k, slot, to):
+        return pltpu.make_async_remote_copy(
+            src_ref=res_ref.at[core, slot], dst_ref=res_ref.at[core, slot],
+            send_sem=g_ssem.at[k], recv_sem=g_rsem.at[slot],
+            device_id={"grp": to * n_core + core}, device_id_type=MESH,
+        )
+
+    def forward_copy(slot, side):
+        return pltpu.make_async_remote_copy(
+            src_ref=res_ref.at[side, slot], dst_ref=res_ref.at[side, slot],
+            send_sem=f_ssem.at[slot], recv_sem=f_rsem.at[slot],
+            device_id={"grp": partner}, device_id_type=MESH,
+        )
+
+    pair_send[...] = product(other).astype(jnp.bfloat16)
+    for k in range(n_z):
+        pair_copy((z + 1 + k) % n_z).start()
+    own_ref[...] = product(core)
+    for k in range(1, n_z):
+        to = (z + k) % n_z
+        pair_copy(to).wait_recv()
+        z_send[to] = (own_ref[to] + pair_recv[to].astype(jnp.float32)).astype(jnp.bfloat16)
+        z_copy(to, z, to).start()
+
+    dd_ref[...] = lax.dot_general(
+        dp_ref[pl.ds(sp, 3)].reshape(-1, channels), pw[...], NT,
+        preferred_element_type=jnp.float32,
+    ).reshape(dd_ref.shape)
+
+    pair_copy(z).wait_recv()
+    mine = own_ref[z] + pair_recv[z].astype(jnp.float32)
+    for k in range(1, n_z):
+        slot = (z + k) % n_z
+        z_copy(slot, slot, z).wait_recv()
+        mine = mine + z_recv[slot].astype(jnp.float32)
+    res_ref[core, z] = mine.astype(jnp.bfloat16)
+    for k in range(1, n_z):
+        gather_copy(k, z, (z + k) % n_z).start()
+    forward_copy(z, core).start()
+
+    for at, lanes in enumerate(blocks):
+        taps = [[dk_ref[i, j : j + 1, lanes] for j in range(3)] for i in range(3)]
+        gain, bias = gain_ref[:, lanes], bias_ref[:, lanes]
+        for b in range(n_samples):
+            own = slice(b * cols, (b + 1) * cols)
+            dd = [dd_ref[i, own, lanes] for i in range(3)]
+            t = [sum(dd[2 - i] * taps[i][j] for i in range(3)) for j in range(3)]
+            dh = t[1] + column_shift(t[0], -1) + column_shift(t[2], 1)
+            a = ga[sp, b, :, lanes].astype(jnp.float32)
+            g = gc[b, sp, :, lanes].astype(jnp.float32)
+            input_grad_ref[b, 0, :, lanes] = (g + jnp.where(a > 0, dh, 0.0)).astype(jnp.bfloat16)
+        for r in range(n_rows):
+            p = p_ref[r, pl.ds(pl.multiple_of(sp * cols, cols), cols), lanes]
+            a = ga[r, sp, :, lanes].astype(jnp.float32)
+            block_out_ref[0, r, :, lanes] = (
+                a + gain * ((p - means[at]) * rstds[at]) + bias
+            ).astype(jnp.bfloat16)
+
+    for k in range(1, n_z):
+        slot = (z + k) % n_z
+        gather_copy(k, slot, z).wait_recv()
+        forward_copy(slot, core).start()
+    for k in range(n_z):
+        forward_copy((z + k) % n_z, other).wait_recv()
+
+    for side in range(n_core):
+        for slot in range(n_z):
+            at = (side * n_z + slot) * part_rows
+            size = min(part_rows, width - at)
+            weight_ref[at : at + size] = res_ref[side, slot, :size].astype(jnp.float32)
+
+    for k in range(1, n_sp):
+        acts_copy(k, sp, (sp + k) % n_sp).wait_send()
+        cot_copy(k, sp, (sp + k) % n_sp).wait_send()
+    for k in range(n_z):
+        pair_copy(k).wait_send()
+        forward_copy(k, core).wait_send()
+    for k in range(1, n_z):
+        z_copy((z + k) % n_z, z, (z + k) % n_z).wait_send()
+        gather_copy(k, z, (z + k) % n_z).wait_send()
+
+
+def fused(acts, cotangent, depth_kernel, point_weight, gain, bias):
+    n_sp, n_grp, n_core = lax.axis_size("sp"), lax.axis_size("grp"), 2
+    n_samples, _, cols, channels = acts.shape
+    n_rows = cotangent.shape[1]
+    n_z = n_grp // n_core
+    width = channels // n_sp
+    part_rows = -(-width // (n_grp * 8)) * 8
+    bf16, f32 = jnp.bfloat16, jnp.float32
+    vmem, dma = pltpu.VMEM, pltpu.SemaphoreType.DMA
+    in_vmem, anywhere = pl.BlockSpec(memory_space=pltpu.VMEM), pl.BlockSpec(memory_space=pl.ANY)
+    rows = n_samples * cols
+    out = pl.pallas_call(
+        functools.partial(kernel, n_sp, n_grp, n_core, part_rows),
+        out_shape=(
+            jax.ShapeDtypeStruct(cotangent.shape, bf16),
+            jax.ShapeDtypeStruct(acts.shape, bf16),
+            jax.ShapeDtypeStruct((width, channels), f32),
+        ),
+        in_specs=[anywhere, anywhere, in_vmem, anywhere, in_vmem, in_vmem],
+        out_specs=(in_vmem, in_vmem, in_vmem),
+        scratch_shapes=[
+            vmem((n_rows, n_samples, cols, channels), bf16),
+            vmem((n_samples, n_rows, cols, channels), bf16),
+            vmem((channels, channels), bf16),
+            vmem((n_rows * rows, channels), bf16),
+            vmem((n_rows, rows, channels), f32),
+            vmem((n_rows + 2, rows, channels), bf16),
+            vmem((n_grp * part_rows, n_rows * rows), bf16),
+            vmem((3, rows, channels), f32),
+            vmem((n_z, part_rows, channels), bf16),
+            vmem((n_z, part_rows, channels), bf16),
+            vmem((n_z, part_rows, channels), f32),
+            vmem((n_z, part_rows, channels), bf16),
+            vmem((n_z, part_rows, channels), bf16),
+            vmem((n_core, n_z, part_rows, channels), bf16),
+            dma((3,)),
+            dma((n_sp,)), dma((n_sp,)), dma((n_sp,)), dma((n_sp,)),
+            dma((n_z,)), dma((n_z,)), dma((n_z,)), dma((n_z,)),
+            dma((n_z,)), dma((n_z,)), dma((n_z,)), dma((n_z,)),
+        ],
+        compiler_params=pltpu.CompilerParams(collective_id=0, has_side_effects=True),
+        name="middle_flow",
+    )(acts, cotangent, depth_kernel, point_weight, gain.reshape(1, -1), bias.reshape(1, -1))
+    return out[0], out[1], out[2].reshape(-1)
 
 
 def depth_forward(field, filter_weight):
@@ -86,7 +372,30 @@
     return (block_out, input_grad, weight_grad)
 
 
+def one_kernel_fits(mesh, acts, cotangent):
+    n_sp, n_grp = mesh.shape["sp"], mesh.shape["grp"]
+    group_elements = acts.size // n_grp
+    return (
+        acts.shape[1] == n_sp
+        and acts.shape[0] == n_sp * n_grp
+        and acts.shape[2] % 16 == 0
+        and acts.shape[3] % n_sp == 0
+        and n_grp % 2 == 0
+        and n_grp > 2
+        and n_sp > 1
+        and group_elements <= 1 << 20
+    )
+
+
 def solution(mesh):
     in_specs = (P("grp", "sp", None, None), P(("grp", "sp"), None, None, None), P(), P(), P(), P())
     out_specs = (P(("grp", "sp"), None, None, None), P("grp", "sp", None, None), P("sp"))
-    return jax.shard_map(body, mesh=mesh, in_specs=in_specs, out_specs=out_specs, check_vma=False)
+
+    def step(acts, cotangent, *params):
+        inner = fused if one_kernel_fits(mesh, acts, cotangent) else body
+        mapped = jax.shard_map(
+            inner, mesh=mesh, in_specs=in_specs, out_specs=out_specs, check_vma=False
+        )
+        return mapped(acts, cotangent, *params)
+
+    return step

time: 161 us -> 36.5 us (0.23)
  waiting for transfers between devices: 102 us -> 0 us
  Pallas kernels: 0 us -> 29.4 us
  blocking collectives: 25.1 us -> 0 us
  between operations: 14.8 us -> 0.66 us
  starting transfers between devices: 5.41 us -> 0 us
  other arithmetic: 4.04 us -> 0 us
    unnamed x3 -> x0, waiting for transfers between devices: 51.5 us -> none
    psum x1 -> x0, waiting for transfers between devices: 47.9 us -> none  [body(): weight_grad = lax.psum(slices, 'grp')]
    pallas_call x0 -> x1, Pallas kernels: none -> 29.4 us  [fused(): pl.pallas_call(functools.partial(kernel, n_sp, n_grp, n_core, part_rows),...]
    psum x2 -> x0, blocking collectives: 17.4 us -> none  [the longest x1 8.99 us: body(): lax.psum((jnp.sum(scaled_output, axis=0), jnp.sum(scaled_output * normali...]
    all_to_all x1 -> x0, blocking collectives: 7.68 us -> none  [body(): lax.all_to_all(dinput, 'sp', split_axis=1, concat_axis=0, tiled=True)]
    all_to_all x1 -> x0, starting transfers between devices: 5.34 us -> none  [body(): lax.all_to_all(acts, 'sp', split_axis=0, concat_axis=1, tiled=True)]
    reshape x0 -> x3, local copies, waits for them, and re-layouts: none -> 4.89 us  [the longest x1 2.36 us: fused(): return (out[0], out[1], out[2].reshape(-1))]
    convert_element_type x1 -> x0, local copies, waits for them, and re-layouts: 3.46 us -> none  [body(): local_weight.astype(jnp.bfloat16)]
  transfers between devices with their start and end apart: 3 -> 0, of which waited for: 3 -> 0; matrix products, arithmetic and copies ran while one was open for 2% -> 0% of each run, Pallas kernels for 0% -> 0%
where the time goes in v1:
time: 36.5 us; the launch traced here: 36.2 us
  Pallas kernels  29.4 us (81%)
  local copies, waits for them, and re-layouts  6.18 us (17%)
  between operations  0.66 us (2%)
    pallas_call x1, Pallas kernels, fused(): pl.pallas_call(functools.partial(kernel, n_sp, n_grp, n_core, part_rows),...  29.4 us
    reshape x1, local copies, waits for them, and re-layouts, fused(): return (out[0], out[1], out[2].reshape(-1))  2.36 us
    unnamed x6, local copies, waits for them, and re-layouts  1.29 us
    reshape x1, local copies, waits for them, and re-layouts, fused(): gain.reshape(1, -1)  1.27 us
    reshape x1, local copies, waits for them, and re-layouts, fused(): bias.reshape(1, -1)  1.27 us

profile of v1, /device:TPU:0, one launch (start us, length us, event | category | flops | bytes accessed | tf_op | source)
XLA Modules:
  0.0 36.2 jit_solution(9657399886626772230)
XLA Ops:
  0.6 1.3 %reshape.15.gain_ref = f32[1,728]{1,0:T(1,128)} reshape(f32[728]{0:T(1024)} %param.10) | data formatting | bytes 5824 | tf_op jit(solution)/shard_map/reshape | solution.py:289
  1.9 1.3 %reshape.16.bias_ref = f32[1,728]{1,0:T(1,128)} reshape(f32[728]{0:T(1024)} %param.11) | data formatting | bytes 5824 | tf_op jit(solution)/shard_map/reshape | solution.py:289
  3.2 29.4 %middle_flow.1 = (bf16[1,4,16,728]{3,2,1,0:T(8,128)(2,1)}, bf16[4,1,16,728]{3,2,1,0:T(8,128)(2,1)}, f32[182,728]{1,0:T(8,128)}) custom-call(bf16[4,1,16,728]{3,2,1,0:T(8,128)(2,1)} %acts_ref.1, bf16[1,4,16,728]{3,2,1,0:T(8,128)(2,1)} %cot_ref.1, f32[3,3,728]{2,1,0:T(4,128)} %dk_ref.1, bf16[728,728]{1,0:T(8,128)(2,1)} %pw_hbm.1, f32[1,728]{1,0:T(1,128)} %reshape.15.gain_ref, ...), custom_call_target="tpu_custom_call" | custom-call | tf_op jit(solution)/shard_map/middle_flow/pallas_call | solution.py:258
  32.6 0.0 copy-start.1
  32.6 0.0 copy-start
  32.6 2.4 %reshape.17 = f32[132496]{0:T(1024)} reshape(f32[182,728]{1,0:T(8,128)} %get-tuple-element.8) | data formatting | bytes 1059968 | tf_op jit(solution)/shard_map/reshape | solution.py:290
  34.9 0.0 copy-done.1
  35.0 0.6 %copy.11 = bf16[1,4,16,728]{3,2,1,0:T(8,128)(2,1)} copy(bf16[1,4,16,728]{3,2,1,0:T(8,128)(2,1)S(1)} %copy-done.1) | data formatting | bytes 186368
  35.6 0.0 copy-done
  35.6 0.6 %copy.12 = bf16[4,1,16,728]{3,2,1,0:T(8,128)(2,1)} copy(bf16[4,1,16,728]{3,2,1,0:T(8,128)(2,1)S(1)} %copy-done) | data formatting | bytes 186368
Async XLA Ops:
  32.6 2.4 %copy-start.1 = (bf16[1,4,16,728]{3,2,1,0:T(8,128)(2,1)S(1)}, bf16[1,4,16,728]{3,2,1,0:T(8,128)(2,1)}, u32[]{:S(2)}) copy-start(bf16[1,4,16,728]{3,2,1,0:T(8,128)(2,1)} %get-tuple-element.12) | copy-start | bytes 279556
  32.6 3.0 %copy-start = (bf16[4,1,16,728]{3,2,1,0:T(8,128)(2,1)S(1)}, bf16[4,1,16,728]{3,2,1,0:T(8,128)(2,1)}, u32[]{:S(2)}) copy-start(bf16[4,1,16,728]{3,2,1,0:T(8,128)(2,1)} %get-tuple-element.13) | copy-start | bytes 279556

commit v2 on v1

--- a/solution.py
+++ b/solution.py
@@ -24,7 +24,7 @@
 
 
 def kernel(
-    n_sp, n_grp, n_core, part_rows,
+    n_sp, n_grp, n_core, n_parts, part_rows,
     acts_ref, cot_ref, dk_ref, pw_hbm, gain_ref, bias_ref,
     block_out_ref, input_grad_ref, weight_ref,
     ga, gc, pw, d_ref, p_ref, dp_ref, dsel_ref, dd_ref,
@@ -38,6 +38,15 @@
     z, core = grp // n_core, grp % n_core
     other = (core + 1) % n_core
     partner = z * n_core + other
+    middle = n_z // 2
+    toward = z + 1 - 2 * (z // middle)
+    away = 2 * z - toward
+    across = (toward // middle - z // middle) * (toward // middle - z // middle)
+    inner = (z > 0) & (z < n_z - 1)
+    side = int(n_sp**0.5)
+    sx = (sp // side) * side + (sp + 1) % side
+    sy = (sp + side) % n_sp
+    far = (sx + side) % n_sp
     n_rows, n_samples, cols, channels = ga.shape
     count = n_rows * n_samples * cols
     blocks = lane_blocks(channels)
@@ -50,38 +59,83 @@
     own_cot.start()
 
     barrier = pltpu.get_barrier_semaphore()
-    peers = [{"sp": (sp + k) % n_sp} for k in range(1, n_sp)]
-    peers += [{"grp": ((z + k) % n_z) * n_core + core} for k in range(1, n_z)]
-    peers += [{"grp": partner}]
+
+    def greet(peer):
+        pl.semaphore_signal(barrier, inc=1, device_id=peer, device_id_type=MESH)
+
+    def z_core(at):
+        return {"grp": at * n_core + core}
+
+    peers = [{"sp": sx}, {"sp": sy}, {"grp": partner}, z_core(toward)]
     for peer in peers:
-        pl.semaphore_signal(barrier, inc=1, device_id=peer, device_id_type=MESH)
-    pl.semaphore_wait(barrier, len(peers))
-
-    def acts_copy(k, slot, to):
-        return pltpu.make_async_remote_copy(
-            src_ref=acts_ref.at[:, 0], dst_ref=ga.at[slot],
-            send_sem=a_send.at[k], recv_sem=a_recv.at[slot],
-            device_id={"sp": to}, device_id_type=MESH,
-        )
-
-    def cot_copy(k, slot, to):
-        return pltpu.make_async_remote_copy(
-            src_ref=cot_ref.at[0], dst_ref=gc.at[slot],
-            send_sem=c_send.at[k], recv_sem=c_recv.at[slot],
-            device_id={"sp": to}, device_id_type=MESH,
-        )
-
-    for k in range(1, n_sp):
-        acts_copy(k, sp, (sp + k) % n_sp).start()
-    for k in range(1, n_sp):
-        cot_copy(k, sp, (sp + k) % n_sp).start()
-
+        greet(peer)
+
+    @pl.when(inner)
+    def _():
+        greet(z_core(away))
+        pl.semaphore_wait(barrier, len(peers) + 1)
+
+    @pl.when(jnp.logical_not(inner))
+    def _():
+        pl.semaphore_wait(barrier, len(peers))
+
+    class Gather:
+        def __init__(self, own, buf, send, recv):
+            self.own, self.buf, self.send, self.recv = own, buf, send, recv
+            self.size = buf.shape[1] // 2
+
+        def part(self, half):
+            return pl.ds(half * self.size, self.size)
+
+        def copy(self, k, src, slot, half, to):
+            return pltpu.make_async_remote_copy(
+                src_ref=src, dst_ref=self.buf.at[slot, self.part(half)],
+                send_sem=self.send.at[k], recv_sem=self.recv.at[slot, half],
+                device_id={"sp": to}, device_id_type=MESH,
+            )
+
+        def direct(self):
+            return [
+                self.copy(k, self.own.at[self.part(half)], sp, half, to)
+                for k, (half, to) in enumerate(((0, sx), (1, sy), (1, sx), (0, sy)))
+            ]
+
+        def relays(self):
+            return [
+                self.copy(4, self.buf.at[sx, self.part(0)], sx, 0, sy),
+                self.copy(5, self.buf.at[sy, self.part(1)], sy, 1, sx),
+            ]
+
+        def arrived(self, slot, half):
+            self.copy(0, self.buf.at[slot, self.part(half)], slot, half, sx).wait_recv()
+
+        def start(self):
+            for copy in self.direct():
+                copy.start()
+
+        def relay(self):
+            for copy, slot, half in zip(self.relays(), (sx, sy), (0, 1)):
+                self.arrived(slot, half)
+                copy.start()
+
+        def finish(self):
+            for slot, half in ((sx, 1), (sy, 0), (far, 0), (far, 1)):
+                self.arrived(slot, half)
+
+        def sent(self):
+            for copy in self.direct() + self.relays():
+                copy.wait_send()
+
+    acts_gather = Gather(acts_ref.at[:, 0], ga, a_send, a_recv)
+    cot_gather = Gather(cot_ref.at[0], gc, c_send, c_recv)
+    acts_gather.start()
     dp_ref[0] = jnp.zeros(dp_ref.shape[1:], dp_ref.dtype)
     dp_ref[n_rows + 1] = jnp.zeros(dp_ref.shape[1:], dp_ref.dtype)
+    acts_gather.relay()
+    cot_gather.start()
     own_acts.wait()
     load_pw.wait()
-    for k in range(1, n_sp):
-        acts_copy(k, (sp + k) % n_sp, sp).wait_recv()
+    acts_gather.finish()
 
     @pl.loop(0, n_samples)
     def _(b):
@@ -97,6 +151,7 @@
                 at = pl.multiple_of((r * n_samples + b) * cols, cols)
                 d_ref[pl.ds(at, cols), lanes] = total.astype(jnp.bfloat16)
 
+    cot_gather.relay()
     p_ref[...] = jnp.dot(
         d_ref[...], pw[...], preferred_element_type=jnp.float32
     ).reshape(p_ref.shape)
@@ -110,8 +165,7 @@
     ).astype(jnp.bfloat16)
 
     own_cot.wait()
-    for k in range(1, n_sp):
-        cot_copy(k, (sp + k) % n_sp, sp).wait_recv()
+    cot_gather.finish()
 
     means, rstds = [], []
     for lanes in blocks:
@@ -123,7 +177,7 @@
                 g = gc[b, r, :, lanes].astype(jnp.float32)
                 s1, s2, sg, sgp = s1 + p, s2 + p * p, sg + g, sgp + g * p
         s1, s2, sg, sgp = [jnp.sum(s, axis=0, keepdims=True) for s in (s1, s2, sg, sgp)]
-        gain = gain_ref[:, lanes]
+        gain = gain_ref[lanes].reshape(1, -1)
         mean = s1 / count
         var = s2 / count - mean * mean
         rstd = lax.rsqrt(var + 1e-05)
@@ -140,13 +194,13 @@
                     rstd * (g * gain - a1 - xhat * a2)
                 ).astype(jnp.bfloat16)
 
-    half = n_z * part_rows
+    half = n_parts * part_rows
 
     def product(which):
         left = dsel_ref[pl.ds(pl.multiple_of(which * half, half), half), :]
         return jnp.dot(
             left, dp_ref[1 : n_rows + 1].reshape(-1, channels), preferred_element_type=jnp.float32
-        ).reshape(n_z, part_rows, channels)
+        ).reshape(n_parts, part_rows, channels)
 
     def pair_copy(k):
         return pltpu.make_async_remote_copy(
@@ -155,56 +209,69 @@
             device_id={"grp": partner}, device_id_type=MESH,
         )
 
-    def z_copy(k, slot, to):
+    def in_copy(k, slot):
         return pltpu.make_async_remote_copy(
-            src_ref=z_send.at[k], dst_ref=z_recv.at[slot],
-            send_sem=z_ssem.at[k], recv_sem=z_rsem.at[slot],
-            device_id={"grp": to * n_core + core}, device_id_type=MESH,
-        )
-
-    def gather_copy(k, slot, to):
+            src_ref=z_send.at[k], dst_ref=z_recv.at[slot, k],
+            send_sem=z_ssem.at[k], recv_sem=z_rsem.at[slot, k],
+            device_id=z_core(toward), device_id_type=MESH,
+        )
+
+    def out_copy(k):
         return pltpu.make_async_remote_copy(
-            src_ref=res_ref.at[core, slot], dst_ref=res_ref.at[core, slot],
-            send_sem=g_ssem.at[k], recv_sem=g_rsem.at[slot],
-            device_id={"grp": to * n_core + core}, device_id_type=MESH,
-        )
-
-    def forward_copy(slot, side):
+            src_ref=res_ref.at[core, k], dst_ref=res_ref.at[core, k],
+            send_sem=g_ssem.at[k], recv_sem=g_rsem.at[k],
+            device_id=z_core(away), device_id_type=MESH,
+        )
+
+    def forward_copy(k, owner):
         return pltpu.make_async_remote_copy(
-            src_ref=res_ref.at[side, slot], dst_ref=res_ref.at[side, slot],
-            send_sem=f_ssem.at[slot], recv_sem=f_rsem.at[slot],
+            src_ref=res_ref.at[owner, k], dst_ref=res_ref.at[owner, k],
+            send_sem=f_ssem.at[k], recv_sem=f_rsem.at[k],
             device_id={"grp": partner}, device_id_type=MESH,
         )
 
     pair_send[...] = product(other).astype(jnp.bfloat16)
-    for k in range(n_z):
-        pair_copy((z + 1 + k) % n_z).start()
+    for k in range(n_parts):
+        pair_copy(k).start()
     own_ref[...] = product(core)
-    for k in range(1, n_z):
-        to = (z + k) % n_z
-        pair_copy(to).wait_recv()
-        z_send[to] = (own_ref[to] + pair_recv[to].astype(jnp.float32)).astype(jnp.bfloat16)
-        z_copy(to, z, to).start()
-
     dd_ref[...] = lax.dot_general(
         dp_ref[pl.ds(sp, 3)].reshape(-1, channels), pw[...], NT,
         preferred_element_type=jnp.float32,
     ).reshape(dd_ref.shape)
 
-    pair_copy(z).wait_recv()
-    mine = own_ref[z] + pair_recv[z].astype(jnp.float32)
-    for k in range(1, n_z):
-        slot = (z + k) % n_z
-        z_copy(slot, slot, z).wait_recv()
-        mine = mine + z_recv[slot].astype(jnp.float32)
-    res_ref[core, z] = mine.astype(jnp.bfloat16)
-    for k in range(1, n_z):
-        gather_copy(k, z, (z + k) % n_z).start()
-    forward_copy(z, core).start()
-
-    for at, lanes in enumerate(blocks):
+    def reduce_in(k):
+        pair_copy(k).wait_recv()
+        own_ref[k] += pair_recv[k].astype(jnp.float32)
+
+        @pl.when(inner)
+        def _():
+            in_copy(k, 0).wait_recv()
+            own_ref[k] += z_recv[0, k].astype(jnp.float32)
+
+        z_send[k] = own_ref[k].astype(jnp.bfloat16)
+        in_copy(k, across).start()
+
+    def spread_out(k):
+        @pl.when(across == 1)
+        def _():
+            in_copy(k, 1).wait_recv()
+            total = z_send[k].astype(jnp.float32) + z_recv[1, k].astype(jnp.float32)
+            res_ref[core, k] = total.astype(jnp.bfloat16)
+
+        @pl.when(across == 0)
+        def _():
+            out_copy(k).wait_recv()
+
+        @pl.when(inner)
+        def _():
+            out_copy(k).start()
+
+        forward_copy(k, core).start()
+
+    def outputs(at):
+        lanes = blocks[at]
         taps = [[dk_ref[i, j : j + 1, lanes] for j in range(3)] for i in range(3)]
-        gain, bias = gain_ref[:, lanes], bias_ref[:, lanes]
+        gain, bias = gain_ref[lanes].reshape(1, -1), bias_ref[lanes].reshape(1, -1)
         for b in range(n_samples):
             own = slice(b * cols, (b + 1) * cols)
             dd = [dd_ref[i, own, lanes] for i in range(3)]
@@ -220,43 +287,52 @@
                 a + gain * ((p - means[at]) * rstds[at]) + bias
             ).astype(jnp.bfloat16)
 
-    for k in range(1, n_z):
-        slot = (z + k) % n_z
-        gather_copy(k, slot, z).wait_recv()
-        forward_copy(slot, core).start()
-    for k in range(n_z):
-        forward_copy((z + k) % n_z, other).wait_recv()
-
-    for side in range(n_core):
-        for slot in range(n_z):
-            at = (side * n_z + slot) * part_rows
-            size = min(part_rows, width - at)
-            weight_ref[at : at + size] = res_ref[side, slot, :size].astype(jnp.float32)
-
-    for k in range(1, n_sp):
-        acts_copy(k, sp, (sp + k) % n_sp).wait_send()
-        cot_copy(k, sp, (sp + k) % n_sp).wait_send()
-    for k in range(n_z):
+    lag = 2
+    for k in range(n_parts + lag):
+        if k < n_parts:
+            reduce_in(k)
+        for at in range(k, len(blocks), n_parts):
+            if k < n_parts:
+                outputs(at)
+        if k >= lag:
+            spread_out(k - lag)
+
+    def write(owner, k):
+        at = (owner * n_parts + k) * part_rows
+        size = min(part_rows, width - at)
+        weight_ref[at : at + size] = res_ref[owner, k, :size].astype(jnp.float32)
+
+    for k in range(n_parts):
+        forward_copy(k, other).wait_recv()
+    for owner in range(n_core):
+        for k in range(n_parts):
+            write(owner, k)
+
+    acts_gather.sent()
+    cot_gather.sent()
+    for k in range(n_parts):
         pair_copy(k).wait_send()
+        in_copy(k, across).wait_send()
         forward_copy(k, core).wait_send()
-    for k in range(1, n_z):
-        z_copy((z + k) % n_z, z, (z + k) % n_z).wait_send()
-        gather_copy(k, z, (z + k) % n_z).wait_send()
+
+        @pl.when(inner)
+        def _():
+            out_copy(k).wait_send()
 
 
 def fused(acts, cotangent, depth_kernel, point_weight, gain, bias):
     n_sp, n_grp, n_core = lax.axis_size("sp"), lax.axis_size("grp"), 2
     n_samples, _, cols, channels = acts.shape
     n_rows = cotangent.shape[1]
-    n_z = n_grp // n_core
+    n_parts = 4
     width = channels // n_sp
-    part_rows = -(-width // (n_grp * 8)) * 8
+    part_rows = -(-width // (n_core * n_parts * 8)) * 8
     bf16, f32 = jnp.bfloat16, jnp.float32
     vmem, dma = pltpu.VMEM, pltpu.SemaphoreType.DMA
     in_vmem, anywhere = pl.BlockSpec(memory_space=pltpu.VMEM), pl.BlockSpec(memory_space=pl.ANY)
     rows = n_samples * cols
     out = pl.pallas_call(
-        functools.partial(kernel, n_sp, n_grp, n_core, part_rows),
+        functools.partial(kernel, n_sp, n_grp, n_core, n_parts, part_rows),
         out_shape=(
             jax.ShapeDtypeStruct(cotangent.shape, bf16),
             jax.ShapeDtypeStruct(acts.shape, bf16),
@@ -271,22 +347,22 @@
             vmem((n_rows * rows, channels), bf16),
             vmem((n_rows, rows, channels), f32),
             vmem((n_rows + 2, rows, channels), bf16),
-            vmem((n_grp * part_rows, n_rows * rows), bf16),
+            vmem((n_core * n_parts * part_rows, n_rows * rows), bf16),
             vmem((3, rows, channels), f32),
-            vmem((n_z, part_rows, channels), bf16),
-            vmem((n_z, part_rows, channels), bf16),
-            vmem((n_z, part_rows, channels), f32),
-            vmem((n_z, part_rows, channels), bf16),
-            vmem((n_z, part_rows, channels), bf16),
-            vmem((n_core, n_z, part_rows, channels), bf16),
+            vmem((n_parts, part_rows, channels), bf16),
+            vmem((n_parts, part_rows, channels), bf16),
+            vmem((n_parts, part_rows, channels), f32),
+            vmem((n_parts, part_rows, channels), bf16),
+            vmem((2, n_parts, part_rows, channels), bf16),
+            vmem((n_core, n_parts, part_rows, channels), bf16),
             dma((3,)),
-            dma((n_sp,)), dma((n_sp,)), dma((n_sp,)), dma((n_sp,)),
-            dma((n_z,)), dma((n_z,)), dma((n_z,)), dma((n_z,)),
-            dma((n_z,)), dma((n_z,)), dma((n_z,)), dma((n_z,)),
+            dma((6,)), dma((n_sp, 2)), dma((6,)), dma((n_sp, 2)),
+            dma((n_parts,)), dma((n_parts,)), dma((n_parts,)), dma((2, n_parts)),
+            dma((n_parts,)), dma((n_parts,)), dma((n_parts,)), dma((n_parts,)),
         ],
         compiler_params=pltpu.CompilerParams(collective_id=0, has_side_effects=True),
         name="middle_flow",
-    )(acts, cotangent, depth_kernel, point_weight, gain.reshape(1, -1), bias.reshape(1, -1))
+    )(acts, cotangent, depth_kernel, point_weight, gain, bias)
     return out[0], out[1], out[2].reshape(-1)
 
 
@@ -380,9 +456,8 @@
         and acts.shape[0] == n_sp * n_grp
         and acts.shape[2] % 16 == 0
         and acts.shape[3] % n_sp == 0
-        and n_grp % 2 == 0
-        and n_grp > 2
-        and n_sp > 1
+        and n_grp % 4 == 0
+        and n_sp == 4
         and group_elements <= 1 << 20
     )
 

time: 36.5 us -> 41.1 us (1.13)
  Pallas kernels: 29.4 us -> 36.6 us
  local copies, waits for them, and re-layouts: 6.18 us -> 3.65 us
    pallas_call x1, Pallas kernels: 29.4 us -> 36.6 us  [fused(): pl.pallas_call(functools.partial(kernel, n_sp, n_grp, n_core, n_parts, pa...]
    reshape x2 -> x0, local copies, waits for them, and re-layouts: 2.53 us -> none  [the longest x1 1.27 us: fused(): gain.reshape(1, -1)]
where the time goes in v2:
time: 41.1 us; the launch traced here: 40.9 us
  Pallas kernels  36.6 us (89%)
  local copies, waits for them, and re-layouts  3.65 us (9%)
  between operations  0.66 us (2%)
    pallas_call x1, Pallas kernels, fused(): pl.pallas_call(functools.partial(kernel, n_sp, n_grp, n_core, n_parts, pa...  36.6 us
    reshape x1, local copies, waits for them, and re-layouts, fused(): return (out[0], out[1], out[2].reshape(-1))  2.36 us
    unnamed x6, local copies, waits for them, and re-layouts  1.29 us

profile of v2, /device:TPU:0, one launch (start us, length us, event | category | flops | bytes accessed | tf_op | source)
XLA Modules:
  0.0 40.9 jit_solution(3447545446590815424)
XLA Ops:
  0.6 36.6 %middle_flow.1 = (bf16[1,4,16,728]{3,2,1,0:T(8,128)(2,1)}, bf16[4,1,16,728]{3,2,1,0:T(8,128)(2,1)}, f32[182,728]{1,0:T(8,128)}) custom-call(bf16[4,1,16,728]{3,2,1,0:T(8,128)(2,1)} %acts_ref.1, bf16[1,4,16,728]{3,2,1,0:T(8,128)(2,1)} %cot_ref.1, f32[3,3,728]{2,1,0:T(4,128)} %dk_ref.1, bf16[728,728]{1,0:T(8,128)(2,1)} %pw_hbm.1, f32[728]{0:T(1024)} %gain_ref.1, ...), custom_call_target="tpu_custom_call" | custom-call | tf_op jit(solution)/shard_map/middle_flow/pallas_call | solution.py:334
  37.3 0.0 copy-start.1
  37.3 0.0 copy-start
  37.3 2.4 %reshape.9 = f32[132496]{0:T(1024)} reshape(f32[182,728]{1,0:T(8,128)} %get-tuple-element.8) | data formatting | bytes 1059968 | tf_op jit(solution)/shard_map/reshape | solution.py:366
  39.7 0.0 copy-done.1
  39.7 0.6 %copy.11 = bf16[1,4,16,728]{3,2,1,0:T(8,128)(2,1)} copy(bf16[1,4,16,728]{3,2,1,0:T(8,128)(2,1)S(1)} %copy-done.1) | data formatting | bytes 186368
  40.3 0.0 copy-done
  40.3 0.6 %copy.12 = bf16[4,1,16,728]{3,2,1,0:T(8,128)(2,1)} copy(bf16[4,1,16,728]{3,2,1,0:T(8,128)(2,1)S(1)} %copy-done) | data formatting | bytes 186368
Async XLA Ops:
  37.3 2.4 %copy-start.1 = (bf16[1,4,16,728]{3,2,1,0:T(8,128)(2,1)S(1)}, bf16[1,4,16,728]{3,2,1,0:T(8,128)(2,1)}, u32[]{:S(2)}) copy-start(bf16[1,4,16,728]{3,2,1,0:T(8,128)(2,1)} %get-tuple-element.12) | copy-start | bytes 279556
  37.3 3.0 %copy-start = (bf16[4,1,16,728]{3,2,1,0:T(8,128)(2,1)S(1)}, bf16[4,1,16,728]{3,2,1,0:T(8,128)(2,1)}, u32[]{:S(2)}) copy-start(bf16[4,1,16,728]{3,2,1,0:T(8,128)(2,1)} %get-tuple-element.13) | copy-start | bytes 279556

commit v3 on v2

--- a/solution.py
+++ b/solution.py
@@ -29,7 +29,7 @@
     block_out_ref, input_grad_ref, weight_ref,
     ga, gc, pw, d_ref, p_ref, dp_ref, dsel_ref, dd_ref,
     pair_send, pair_recv, own_ref, z_send, z_recv, res_ref,
-    local_sem, a_send, a_recv, c_send, c_recv,
+    local_sem, ready, a_send, a_recv, c_send, c_recv,
     pair_ssem, pair_rsem, z_ssem, z_rsem, g_ssem, g_rsem, f_ssem, f_rsem,
 ):
     sp = lax.axis_index("sp")
@@ -41,7 +41,6 @@
     middle = n_z // 2
     toward = z + 1 - 2 * (z // middle)
     away = 2 * z - toward
-    across = (toward // middle - z // middle) * (toward // middle - z // middle)
     inner = (z > 0) & (z < n_z - 1)
     side = int(n_sp**0.5)
     sx = (sp // side) * side + (sp + 1) % side
@@ -100,6 +99,14 @@
                 for k, (half, to) in enumerate(((0, sx), (1, sy), (1, sx), (0, sy)))
             ]
 
+        def start_relayed(self):
+            for copy in self.direct()[:2]:
+                copy.start()
+
+        def start_rest(self):
+            for copy in self.direct()[2:]:
+                copy.start()
+
         def relays(self):
             return [
                 self.copy(4, self.buf.at[sx, self.part(0)], sx, 0, sy),
@@ -109,10 +116,6 @@
         def arrived(self, slot, half):
             self.copy(0, self.buf.at[slot, self.part(half)], slot, half, sx).wait_recv()
 
-        def start(self):
-            for copy in self.direct():
-                copy.start()
-
         def relay(self):
             for copy, slot, half in zip(self.relays(), (sx, sy), (0, 1)):
                 self.arrived(slot, half)
@@ -128,13 +131,34 @@
 
     acts_gather = Gather(acts_ref.at[:, 0], ga, a_send, a_recv)
     cot_gather = Gather(cot_ref.at[0], gc, c_send, c_recv)
-    acts_gather.start()
+    acts_gather.start_relayed()
+    acts_gather.start_rest()
+    cot_gather.start_relayed()
     dp_ref[0] = jnp.zeros(dp_ref.shape[1:], dp_ref.dtype)
     dp_ref[n_rows + 1] = jnp.zeros(dp_ref.shape[1:], dp_ref.dtype)
     acts_gather.relay()
-    cot_gather.start()
+    cot_gather.start_rest()
+    for level in range(n_z - 2):
+        for step in (1, -1):
+            there = (z + step >= 0) & (z + step < n_z)
+
+            @pl.when(there)
+            def _():
+                pl.semaphore_signal(
+                    ready.at[level, (1 - step) // 2], inc=1,
+                    device_id=z_core(z + step), device_id_type=MESH,
+                )
+
+        for step in (1, -1):
+            there = (z + step >= 0) & (z + step < n_z)
+
+            @pl.when(there)
+            def _():
+                pl.semaphore_wait(ready.at[level, (1 + step) // 2], 1)
+
     own_acts.wait()
     load_pw.wait()
+    cot_gather.relay()
     acts_gather.finish()
 
     @pl.loop(0, n_samples)
@@ -151,7 +175,6 @@
                 at = pl.multiple_of((r * n_samples + b) * cols, cols)
                 d_ref[pl.ds(at, cols), lanes] = total.astype(jnp.bfloat16)
 
-    cot_gather.relay()
     p_ref[...] = jnp.dot(
         d_ref[...], pw[...], preferred_element_type=jnp.float32
     ).reshape(p_ref.shape)
@@ -209,18 +232,18 @@
             device_id={"grp": partner}, device_id_type=MESH,
         )
 
-    def in_copy(k, slot):
+    def z_copy(k, slot, to):
         return pltpu.make_async_remote_copy(
-            src_ref=z_send.at[k], dst_ref=z_recv.at[slot, k],
-            send_sem=z_ssem.at[k], recv_sem=z_rsem.at[slot, k],
-            device_id=z_core(toward), device_id_type=MESH,
-        )
-
-    def out_copy(k):
+            src_ref=z_send.at[k], dst_ref=z_recv.at[slot],
+            send_sem=z_ssem.at[k], recv_sem=z_rsem.at[slot],
+            device_id=z_core(to), device_id_type=MESH,
+        )
+
+    def gather_copy(k, slot, to):
         return pltpu.make_async_remote_copy(
-            src_ref=res_ref.at[core, k], dst_ref=res_ref.at[core, k],
-            send_sem=g_ssem.at[k], recv_sem=g_rsem.at[k],
-            device_id=z_core(away), device_id_type=MESH,
+            src_ref=res_ref.at[core, slot], dst_ref=res_ref.at[core, slot],
+            send_sem=g_ssem.at[k], recv_sem=g_rsem.at[slot],
+            device_id=z_core(to), device_id_type=MESH,
         )
 
     def forward_copy(k, owner):
@@ -229,44 +252,6 @@
             send_sem=f_ssem.at[k], recv_sem=f_rsem.at[k],
             device_id={"grp": partner}, device_id_type=MESH,
         )
-
-    pair_send[...] = product(other).astype(jnp.bfloat16)
-    for k in range(n_parts):
-        pair_copy(k).start()
-    own_ref[...] = product(core)
-    dd_ref[...] = lax.dot_general(
-        dp_ref[pl.ds(sp, 3)].reshape(-1, channels), pw[...], NT,
-        preferred_element_type=jnp.float32,
-    ).reshape(dd_ref.shape)
-
-    def reduce_in(k):
-        pair_copy(k).wait_recv()
-        own_ref[k] += pair_recv[k].astype(jnp.float32)
-
-        @pl.when(inner)
-        def _():
-            in_copy(k, 0).wait_recv()
-            own_ref[k] += z_recv[0, k].astype(jnp.float32)
-
-        z_send[k] = own_ref[k].astype(jnp.bfloat16)
-        in_copy(k, across).start()
-
-    def spread_out(k):
-        @pl.when(across == 1)
-        def _():
-            in_copy(k, 1).wait_recv()
-            total = z_send[k].astype(jnp.float32) + z_recv[1, k].astype(jnp.float32)
-            res_ref[core, k] = total.astype(jnp.bfloat16)
-
-        @pl.when(across == 0)
-        def _():
-            out_copy(k).wait_recv()
-
-        @pl.when(inner)
-        def _():
-            out_copy(k).start()
-
-        forward_copy(k, core).start()
 
     def outputs(at):
         lanes = blocks[at]
@@ -287,44 +272,65 @@
                 a + gain * ((p - means[at]) * rstds[at]) + bias
             ).astype(jnp.bfloat16)
 
-    lag = 2
-    for k in range(n_parts + lag):
-        if k < n_parts:
-            reduce_in(k)
-        for at in range(k, len(blocks), n_parts):
-            if k < n_parts:
-                outputs(at)
-        if k >= lag:
-            spread_out(k - lag)
-
     def write(owner, k):
         at = (owner * n_parts + k) * part_rows
         size = min(part_rows, width - at)
         weight_ref[at : at + size] = res_ref[owner, k, :size].astype(jnp.float32)
 
-    for k in range(n_parts):
-        forward_copy(k, other).wait_recv()
+    pair_send[...] = product(other).astype(jnp.bfloat16)
+    for k in range(1, n_z + 1):
+        pair_copy((z + k) % n_z).start()
+    own_ref[...] = product(core)
+    for k in range(1, n_z):
+        to = (z + k) % n_z
+        pair_copy(to).wait_recv()
+        z_send[to] = (own_ref[to] + pair_recv[to].astype(jnp.float32)).astype(jnp.bfloat16)
+        z_copy(to, z, to).start()
+
+    dd_ref[...] = lax.dot_general(
+        dp_ref[pl.ds(sp, 3)].reshape(-1, channels), pw[...], NT,
+        preferred_element_type=jnp.float32,
+    ).reshape(dd_ref.shape)
+
+    pair_copy(z).wait_recv()
+    mine = own_ref[z] + pair_recv[z].astype(jnp.float32)
+    for k in range(1, n_z):
+        slot = (z + k) % n_z
+        z_copy(slot, slot, z).wait_recv()
+        mine = mine + z_recv[slot].astype(jnp.float32)
+    res_ref[core, z] = mine.astype(jnp.bfloat16)
+    for k in range(1, n_z):
+        gather_copy(k, z, (z + k) % n_z).start()
+    forward_copy(z, core).start()
+
+    for at in range(len(blocks)):
+        outputs(at)
+
+    for k in range(1, n_z):
+        slot = (z + k) % n_z
+        gather_copy(k, slot, z).wait_recv()
+        forward_copy(slot, core).start()
+    for k in range(n_z):
+        forward_copy((z + k) % n_z, other).wait_recv()
     for owner in range(n_core):
-        for k in range(n_parts):
+        for k in range(n_z):
             write(owner, k)
 
     acts_gather.sent()
     cot_gather.sent()
-    for k in range(n_parts):
+    for k in range(n_z):
         pair_copy(k).wait_send()
-        in_copy(k, across).wait_send()
         forward_copy(k, core).wait_send()
-
-        @pl.when(inner)
-        def _():
-            out_copy(k).wait_send()
+    for k in range(1, n_z):
+        z_copy((z + k) % n_z, z, (z + k) % n_z).wait_send()
+        gather_copy(k, z, (z + k) % n_z).wait_send()
 
 
 def fused(acts, cotangent, depth_kernel, point_weight, gain, bias):
     n_sp, n_grp, n_core = lax.axis_size("sp"), lax.axis_size("grp"), 2
     n_samples, _, cols, channels = acts.shape
     n_rows = cotangent.shape[1]
-    n_parts = 4
+    n_parts = n_grp // n_core
     width = channels // n_sp
     part_rows = -(-width // (n_core * n_parts * 8)) * 8
     bf16, f32 = jnp.bfloat16, jnp.float32
@@ -353,11 +359,12 @@
             vmem((n_parts, part_rows, channels), bf16),
             vmem((n_parts, part_rows, channels), f32),
             vmem((n_parts, part_rows, channels), bf16),
-            vmem((2, n_parts, part_rows, channels), bf16),
+            vmem((n_parts, part_rows, channels), bf16),
             vmem((n_core, n_parts, part_rows, channels), bf16),
             dma((3,)),
+            pltpu.SemaphoreType.REGULAR((n_parts - 2, 2)),
             dma((6,)), dma((n_sp, 2)), dma((6,)), dma((n_sp, 2)),
-            dma((n_parts,)), dma((n_parts,)), dma((n_parts,)), dma((2, n_parts)),
+            dma((n_parts,)), dma((n_parts,)), dma((n_parts,)), dma((n_parts,)),
             dma((n_parts,)), dma((n_parts,)), dma((n_parts,)), dma((n_parts,)),
         ],
         compiler_params=pltpu.CompilerParams(collective_id=0, has_side_effects=True),

time: 41.1 us -> 32.5 us (0.79)
  Pallas kernels: 36.6 us -> 28 us
    pallas_call x1, Pallas kernels: 36.6 us -> 28 us  [fused(): pl.pallas_call(functools.partial(kernel, n_sp, n_grp, n_core, n_parts, pa...]
where the time goes in v3:
time: 32.5 us; the launch traced here: 32.3 us
  Pallas kernels  28 us (86%)
  local copies, waits for them, and re-layouts  3.65 us (11%)
  between operations  0.66 us (2%)
    pallas_call x1, Pallas kernels, fused(): pl.pallas_call(functools.partial(kernel, n_sp, n_grp, n_core, n_parts, pa...  28 us
    reshape x1, local copies, waits for them, and re-layouts, fused(): return (out[0], out[1], out[2].reshape(-1))  2.36 us
    unnamed x6, local copies, waits for them, and re-layouts  1.29 us

profile of v3, /device:TPU:0, one launch (start us, length us, event | category | flops | bytes accessed | tf_op | source)
XLA Modules:
  0.0 32.3 jit_solution(3674935580796906455)
XLA Ops:
  0.6 28.0 %middle_flow.1 = (bf16[1,4,16,728]{3,2,1,0:T(8,128)(2,1)}, bf16[4,1,16,728]{3,2,1,0:T(8,128)(2,1)}, f32[182,728]{1,0:T(8,128)}) custom-call(bf16[4,1,16,728]{3,2,1,0:T(8,128)(2,1)} %acts_ref.1, bf16[1,4,16,728]{3,2,1,0:T(8,128)(2,1)} %cot_ref.1, f32[3,3,728]{2,1,0:T(4,128)} %dk_ref.1, bf16[728,728]{1,0:T(8,128)(2,1)} %pw_hbm.1, f32[728]{0:T(1024)} %gain_ref.1, ...), custom_call_target="tpu_custom_call" | custom-call | tf_op jit(solution)/shard_map/middle_flow/pallas_call | solution.py:340
  28.6 0.0 copy-start.1
  28.6 0.0 copy-start
  28.6 2.4 %reshape.9 = f32[132496]{0:T(1024)} reshape(f32[182,728]{1,0:T(8,128)} %get-tuple-element.8) | data formatting | bytes 1059968 | tf_op jit(solution)/shard_map/reshape | solution.py:373
  31.0 0.0 copy-done.1
  31.0 0.6 %copy.11 = bf16[1,4,16,728]{3,2,1,0:T(8,128)(2,1)} copy(bf16[1,4,16,728]{3,2,1,0:T(8,128)(2,1)S(1)} %copy-done.1) | data formatting | bytes 186368
  31.6 0.0 copy-done
  31.6 0.6 %copy.12 = bf16[4,1,16,728]{3,2,1,0:T(8,128)(2,1)} copy(bf16[4,1,16,728]{3,2,1,0:T(8,128)(2,1)S(1)} %copy-done) | data formatting | bytes 186368
Async XLA Ops:
  28.6 2.4 %copy-start.1 = (bf16[1,4,16,728]{3,2,1,0:T(8,128)(2,1)S(1)}, bf16[1,4,16,728]{3,2,1,0:T(8,128)(2,1)}, u32[]{:S(2)}) copy-start(bf16[1,4,16,728]{3,2,1,0:T(8,128)(2,1)} %get-tuple-element.12) | copy-start | bytes 279556
  28.6 3.0 %copy-start = (bf16[4,1,16,728]{3,2,1,0:T(8,128)(2,1)S(1)}, bf16[4,1,16,728]{3,2,1,0:T(8,128)(2,1)}, u32[]{:S(2)}) copy-start(bf16[4,1,16,728]{3,2,1,0:T(8,128)(2,1)} %get-tuple-element.13) | copy-start | bytes 279556

commit v4 on v3

--- a/solution.py
+++ b/solution.py
@@ -1,4 +1,5 @@
 import functools
+import math
 
 import jax
 import jax.numpy as jnp
@@ -28,7 +29,7 @@
     acts_ref, cot_ref, dk_ref, pw_hbm, gain_ref, bias_ref,
     block_out_ref, input_grad_ref, weight_ref,
     ga, gc, pw, d_ref, p_ref, dp_ref, dsel_ref, dd_ref,
-    pair_send, pair_recv, own_ref, z_send, z_recv, res_ref,
+    pair_send, pair_recv, own_ref, z_send, z_recv, res_ref, flat_rows,
     local_sem, ready, a_send, a_recv, c_send, c_recv,
     pair_ssem, pair_rsem, z_ssem, z_rsem, g_ssem, g_rsem, f_ssem, f_rsem,
 ):
@@ -134,6 +135,7 @@
     acts_gather.start_relayed()
     acts_gather.start_rest()
     cot_gather.start_relayed()
+    flat_rows[...] = jnp.zeros(flat_rows.shape, flat_rows.dtype)
     dp_ref[0] = jnp.zeros(dp_ref.shape[1:], dp_ref.dtype)
     dp_ref[n_rows + 1] = jnp.zeros(dp_ref.shape[1:], dp_ref.dtype)
     acts_gather.relay()
@@ -274,8 +276,34 @@
 
     def write(owner, k):
         at = (owner * n_parts + k) * part_rows
-        size = min(part_rows, width - at)
-        weight_ref[at : at + size] = res_ref[owner, k, :size].astype(jnp.float32)
+        for c, lanes in enumerate(blocks):
+            size = lanes.stop - lanes.start
+            flat_rows[c, at : at + part_rows, :size] = res_ref[owner, k, :, lanes].astype(
+                jnp.float32
+            )
+
+    def flatten():
+        period = LANES // math.gcd(channels, LANES)
+        step = channels * period // LANES
+        runs = flat_rows.shape[1] // period
+        at = lax.broadcasted_iota(jnp.int32, (runs, LANES), 1)
+        last = None
+        for r in range(period):
+            row, shift = divmod(channels * r, LANES)
+            parts = [flat_rows[c, pl.ds(r, runs, stride=period), :] for c in range(len(blocks))]
+            if shift:
+                parts = [pltpu.roll(part, shift, 1) for part in parts]
+                zero = jnp.zeros((runs, LANES), jnp.float32)
+                parts = [
+                    jnp.where(at < shift, before, part)
+                    for before, part in zip([zero] + parts, parts + [zero])
+                ]
+                parts[0] = parts[0] + last
+            used = -(-(shift + channels) // LANES)
+            ends = (shift + channels) % LANES == 0
+            for c in range(used if ends else used - 1):
+                weight_ref[pl.ds(row + c, runs, stride=step), :] = parts[c]
+            last = parts[used - 1]
 
     pair_send[...] = product(other).astype(jnp.bfloat16)
     for k in range(1, n_z + 1):
@@ -315,6 +343,7 @@
     for owner in range(n_core):
         for k in range(n_z):
             write(owner, k)
+    flatten()
 
     acts_gather.sent()
     cot_gather.sent()
@@ -333,6 +362,8 @@
     n_parts = n_grp // n_core
     width = channels // n_sp
     part_rows = -(-width // (n_core * n_parts * 8)) * 8
+    period = LANES // math.gcd(channels, LANES)
+    padded = -(-n_core * n_parts * part_rows // period) * period
     bf16, f32 = jnp.bfloat16, jnp.float32
     vmem, dma = pltpu.VMEM, pltpu.SemaphoreType.DMA
     in_vmem, anywhere = pl.BlockSpec(memory_space=pltpu.VMEM), pl.BlockSpec(memory_space=pl.ANY)
@@ -342,7 +373,7 @@
         out_shape=(
             jax.ShapeDtypeStruct(cotangent.shape, bf16),
             jax.ShapeDtypeStruct(acts.shape, bf16),
-            jax.ShapeDtypeStruct((width, channels), f32),
+            jax.ShapeDtypeStruct((padded * channels // LANES, LANES), f32),
         ),
         in_specs=[anywhere, anywhere, in_vmem, anywhere, in_vmem, in_vmem],
         out_specs=(in_vmem, in_vmem, in_vmem),
@@ -361,6 +392,7 @@
             vmem((n_parts, part_rows, channels), bf16),
             vmem((n_parts, part_rows, channels), bf16),
             vmem((n_core, n_parts, part_rows, channels), bf16),
+            vmem((len(lane_blocks(channels)), padded, LANES), f32),
             dma((3,)),
             pltpu.SemaphoreType.REGULAR((n_parts - 2, 2)),
             dma((6,)), dma((n_sp, 2)), dma((6,)), dma((n_sp, 2)),
@@ -370,7 +402,7 @@
         compiler_params=pltpu.CompilerParams(collective_id=0, has_side_effects=True),
         name="middle_flow",
     )(acts, cotangent, depth_kernel, point_weight, gain, bias)
-    return out[0], out[1], out[2].reshape(-1)
+    return out[0], out[1], out[2].reshape(-1)[: width * channels]
 
 
 def depth_forward(field, filter_weight):

time: 32.5 us -> 32.2 us (level)
  local copies, waits for them, and re-layouts: 3.65 us -> 3.2 us
    reshape x1 -> x0, local copies, waits for them, and re-layouts: 2.36 us -> none  [fused(): return (out[0], out[1], out[2].reshape(-1))]
    slice x0 -> x1, local copies, waits for them, and re-layouts: none -> 1.91 us  [fused(): return (out[0], out[1], out[2].reshape(-1)[:width * channels])]
where the time goes in v4:
time: 32.2 us; the launch traced here: 31.8 us
  Pallas kernels  28 us (87%)
  local copies, waits for them, and re-layouts  3.2 us (10%)
  between operations  0.66 us (2%)
    pallas_call x1, Pallas kernels, fused(): pl.pallas_call(functools.partial(kernel, n_sp, n_grp, n_core, n_parts, pa...  28 us
    slice x1, local copies, waits for them, and re-layouts, fused(): return (out[0], out[1], out[2].reshape(-1)[:width * channels])  1.91 us
    unnamed x6, local copies, waits for them, and re-layouts  1.29 us

profile of v4, /device:TPU:0, one launch (start us, length us, event | category | flops | bytes accessed | tf_op | source)
XLA Modules:
  0.0 31.8 jit_solution(7932610528643097492)
XLA Ops:
  0.6 28.0 %middle_flow.1 = (bf16[1,4,16,728]{3,2,1,0:T(8,128)(2,1)}, bf16[4,1,16,728]{3,2,1,0:T(8,128)(2,1)}, f32[1092,128]{1,0:T(8,128)}) custom-call(bf16[4,1,16,728]{3,2,1,0:T(8,128)(2,1)} %acts_ref.1, bf16[1,4,16,728]{3,2,1,0:T(8,128)(2,1)} %cot_ref.1, f32[3,3,728]{2,1,0:T(4,128)} %dk_ref.1, bf16[728,728]{1,0:T(8,128)(2,1)} %pw_hbm.1, f32[728]{0:T(1024)} %gain_ref.1, ...), custom_call_target="tpu_custom_call" | custom-call | tf_op jit(solution)/shard_map/middle_flow/pallas_call | solution.py:371
  28.6 0.0 copy-start.1
  28.6 0.0 copy-start
  28.6 1.9 %slice.4 = f32[132496]{0:T(1024)} slice(f32[139776]{0:T(1024)} %bitcast.1), slice={[0:132496]} | slice | bytes 1059968 | tf_op jit(solution)/shard_map/slice | solution.py:405
  30.5 0.0 copy-done.1
  30.5 0.6 %copy.11 = bf16[1,4,16,728]{3,2,1,0:T(8,128)(2,1)} copy(bf16[1,4,16,728]{3,2,1,0:T(8,128)(2,1)S(1)} %copy-done.1) | data formatting | bytes 186368
  31.2 0.0 copy-done
  31.2 0.6 %copy.12 = bf16[4,1,16,728]{3,2,1,0:T(8,128)(2,1)} copy(bf16[4,1,16,728]{3,2,1,0:T(8,128)(2,1)S(1)} %copy-done) | data formatting | bytes 186368
Async XLA Ops:
  28.6 1.9 %copy-start.1 = (bf16[1,4,16,728]{3,2,1,0:T(8,128)(2,1)S(1)}, bf16[1,4,16,728]{3,2,1,0:T(8,128)(2,1)}, u32[]{:S(2)}) copy-start(bf16[1,4,16,728]{3,2,1,0:T(8,128)(2,1)} %get-tuple-element.12) | copy-start | bytes 279556
  28.6 2.6 %copy-start = (bf16[4,1,16,728]{3,2,1,0:T(8,128)(2,1)S(1)}, bf16[4,1,16,728]{3,2,1,0:T(8,128)(2,1)}, u32[]{:S(2)}) copy-start(bf16[4,1,16,728]{3,2,1,0:T(8,128)(2,1)} %get-tuple-element.13) | copy-start | bytes 279556

commit v5 on v4

--- a/solution.py
+++ b/solution.py
@@ -353,6 +353,16 @@
     for k in range(1, n_z):
         z_copy((z + k) % n_z, z, (z + k) % n_z).wait_send()
         gather_copy(k, z, (z + k) % n_z).wait_send()
+
+
+def finish(block_ref, grad_ref, weight_ref, block_out_ref, grad_out_ref, flat_ref):
+    block_out_ref[...] = block_ref[...]
+    grad_out_ref[...] = grad_ref[...]
+    size, tile = flat_ref.shape[0], 8 * LANES
+    for at in range(0, size, tile):
+        part = weight_ref[at // LANES : at // LANES + 8].reshape(tile)
+        left = min(tile, size - at)
+        flat_ref[at : at + left] = part[:left]
 
 
 def fused(acts, cotangent, depth_kernel, point_weight, gain, bias):
@@ -402,7 +412,17 @@
         compiler_params=pltpu.CompilerParams(collective_id=0, has_side_effects=True),
         name="middle_flow",
     )(acts, cotangent, depth_kernel, point_weight, gain, bias)
-    return out[0], out[1], out[2].reshape(-1)[: width * channels]
+    return pl.pallas_call(
+        finish,
+        out_shape=(
+            jax.ShapeDtypeStruct(cotangent.shape, bf16),
+            jax.ShapeDtypeStruct(acts.shape, bf16),
+            jax.ShapeDtypeStruct((width * channels,), f32),
+        ),
+        in_specs=[in_vmem, in_vmem, in_vmem],
+        out_specs=(in_vmem, in_vmem, in_vmem),
+        name="finish",
+    )(*out)
 
 
 def depth_forward(field, filter_weight):

time: 32.2 us -> 31 us (0.963)
  local copies, waits for them, and re-layouts: 3.2 us -> 0 us
  Pallas kernels: 28 us -> 30 us
    pallas_call x0 -> x1, Pallas kernels: none -> 2.03 us  [fused(): pl.pallas_call(finish, out_shape=(jax.ShapeDtypeStruct(cotangent.shape, b...]
    slice x1 -> x0, local copies, waits for them, and re-layouts: 1.91 us -> none  [fused(): return (out[0], out[1], out[2].reshape(-1)[:width * channels])]
    unnamed x6 -> x0, local copies, waits for them, and re-layouts: 1.29 us -> none
where the time goes in v5:
time: 31 us; the launch traced here: 30.6 us
  Pallas kernels  30 us (97%)
  between operations  0.64 us (2%)
    pallas_call x1, Pallas kernels, fused(): pl.pallas_call(functools.partial(kernel, n_sp, n_grp, n_core, n_parts, pa...  28 us
    pallas_call x1, Pallas kernels, fused(): pl.pallas_call(finish, out_shape=(jax.ShapeDtypeStruct(cotangent.shape, b...  2.03 us

profile of v5, /device:TPU:0, one launch (start us, length us, event | category | flops | bytes accessed | tf_op | source)
XLA Modules:
  0.0 30.6 jit_solution(14018850582905232958)
XLA Ops:
  0.6 28.0 %middle_flow.1 = (bf16[1,4,16,728]{3,2,1,0:T(8,128)(2,1)}, bf16[4,1,16,728]{3,2,1,0:T(8,128)(2,1)}, f32[1092,128]{1,0:T(8,128)}) custom-call(bf16[4,1,16,728]{3,2,1,0:T(8,128)(2,1)} %acts_ref.1, bf16[1,4,16,728]{3,2,1,0:T(8,128)(2,1)} %cot_ref.1, f32[3,3,728]{2,1,0:T(4,128)} %dk_ref.1, bf16[728,728]{1,0:T(8,128)(2,1)} %pw_hbm.1, f32[728]{0:T(1024)} %gain_ref.1, ...), custom_call_target="tpu_custom_call" | custom-call | tf_op jit(solution)/shard_map/middle_flow/pallas_call | solution.py:381
  28.6 2.0 %finish.1 = (bf16[1,4,16,728]{3,2,1,0:T(8,128)(2,1)}, bf16[4,1,16,728]{3,2,1,0:T(8,128)(2,1)}, f32[132496]{0:T(1024)}) custom-call(bf16[1,4,16,728]{3,2,1,0:T(8,128)(2,1)} %get-tuple-element.6.block_ref, bf16[4,1,16,728]{3,2,1,0:T(8,128)(2,1)} %get-tuple-element.7.grad_ref, f32[1092,128]{1,0:T(8,128)} %get-tuple-element.8.weight_ref), custom_call_target="tpu_custom_call" | custom-call | tf_op jit(solution)/shard_map/finish/pallas_call | solution.py:415
